TPU v7x, 128 devices: a whole 4x4x4 slice. The times are simulated.
128 devices in a mesh: dp: 16 (over z, y), tensor: 8 (over x, core).
Axes of the slice: x: 4, y: 4, z: 4, core: 2. Of those that a mesh axis runs over, the one named last changes fastest.
Arguments:
- dense: bfloat16 [3072, 2048], P('dp'), may hold values from -8 to 8
- bottom_weight: bfloat16 [2048, 16384], P(None, 'tensor'), may hold values from -0.125 to 0.125
- bottom_bias: float32 [16384], P('tensor'), may hold values from -3 to 3
- cross_blocks: bfloat16 [80, 512, 512], P('tensor', 'dp'), may hold values from -0.25 to 0.25
- cross_bias: float32 [16384], P('tensor'), may hold values from -3 to 3
- cotangent: bfloat16 [3072, 16384], P('dp', 'tensor'), may hold values from -6 to 6
- in_blocks: int32 [8, 10], replicated, may hold values from 0 to 31, as said below
- out_blocks: int32 [8, 10], replicated, may hold values from 0 to 31, as said below
- live_slots: int32 [8], replicated, may hold values from 2 to 10, as said below
Outputs:
- cross_out: bfloat16 [3072, 16384], P('dp', 'tensor')
- grad_bottom: float32 [2048, 16384], P('dp', 'tensor')
- grad_bias_bottom: float32 [16384], P('tensor')
- grad_blocks: float32 [80, 512, 512], P('tensor', 'dp')
- grad_bias: float32 [16384], P('tensor')
Inputs may be any that keep to these rules, and one draw needn't show every extreme that they name: `in_blocks`: among the live slots of one tensor device, at most 2 have input blocks held by any one tensor device (blocks s * 16384 / (512 * 8) onward for device s), and this most is reached in every draw. `out_blocks`: among the live slots of one tensor device, at most 2 have output blocks held by any one tensor device, and this most is reached in every draw. `live_slots`: some tensor device has all 10 slots live.
All inputs are finite; a program needn't handle non-finite values.
Results may differ from a plain program's by a relative error of at most 0.014.
Values may be sent and summed in bfloat16 or wider, within the bound.
A program may use at most 128 MiB of HBM per device.

v0:
```python
import jax
import jax.numpy as jnp
from jax import lax
from jax.sharding import PartitionSpec as P

BLK = 512
SLOTS = 10


def slot_ranks(owner, alive):
    order = jnp.arange(owner.shape[1])
    earlier = order[None, :] < order[:, None]
    same = (owner[:, :, None] == owner[:, None, :]) & alive[:, None, :] & earlier[None, :, :]
    return jnp.sum(same.astype(jnp.int32), axis=2)


def post_table(owner_mine, rank_mine, alive_mine, groups, capacity):
    slot_count = owner_mine.shape[0]
    match = (
        (owner_mine[None, None, :] == jnp.arange(groups)[:, None, None])
        & (rank_mine[None, None, :] == jnp.arange(capacity)[None, :, None])
        & alive_mine[None, None, :]
    )
    chosen = jnp.sum(match.astype(jnp.int32) * jnp.arange(slot_count)[None, None, :], axis=2)
    filled = jnp.any(match, axis=2)
    return (chosen, filled)


def pack_parts(parts, chosen, filled):
    picked = jnp.take(parts, chosen.reshape(-1), axis=1) * filled.reshape(-1)[None, :, None].astype(
        parts.dtype
    )
    return picked.reshape(parts.shape[0], chosen.shape[0], chosen.shape[1] * parts.shape[2])


def collect_parts(received, owner, local, rank, alive, target, capacity, per_device):
    row_count, groups, span_width = received.shape
    block_width = span_width // capacity
    match = ((owner == target) & alive)[:, :, None] & (
        rank[:, :, None] == jnp.arange(capacity)[None, None, :]
    )
    matches = match[:, :, :, None] & (
        local[:, :, None, None] == jnp.arange(per_device)[None, None, None, :]
    )
    onehot = (
        jnp.sum(matches.astype(jnp.int32), axis=1)
        .reshape(groups * capacity, per_device)
        .astype(jnp.bfloat16)
    )
    flattened = received.reshape(row_count, groups * capacity, block_width)
    summed = jnp.einsum("rib,il->rlb", flattened, onehot, preferred_element_type=jnp.float32)
    return summed.reshape(row_count, per_device * block_width)


def on_device(
    dense,
    bottom_weight,
    bottom_bias,
    cross_blocks,
    cross_bias,
    cotangent,
    in_blocks,
    out_blocks,
    live_slots,
):
    groups = lax.axis_size("tensor")
    mine = lax.axis_index("tensor")
    row_count = dense.shape[0]
    local_width = bottom_weight.shape[1]
    per_device = local_width // BLK
    capacity = -(-SLOTS // groups)
    preact = jnp.dot(dense, bottom_weight, preferred_element_type=jnp.float32) + bottom_bias
    start = jax.nn.silu(preact).astype(jnp.bfloat16)
    start_wide = start.astype(jnp.float32)
    cot_wide = cotangent.astype(jnp.float32)
    grad_mixed = cot_wide * start_wide
    grad_mixed_low = grad_mixed.astype(jnp.bfloat16)
    alive = jnp.arange(SLOTS)[None, :] < live_slots[:, None]
    alive_mine = alive[mine]
    switch = alive_mine.astype(jnp.bfloat16)[None, :, None]
    in_owner = in_blocks // per_device
    in_local = in_blocks % per_device
    out_owner = out_blocks // per_device
    out_local = out_blocks % per_device
    in_rank = slot_ranks(in_owner, alive)
    out_rank = slot_ranks(out_owner, alive)
    whole_start = lax.all_gather(start, "tensor", axis=1, tiled=True)
    fetched = jnp.take(whole_start.reshape(row_count, -1, BLK), in_blocks[mine], axis=1)
    taken = fetched
    product = jnp.einsum(
        "rki,kij->rkj",
        taken,
        lax.all_gather(cross_blocks, "dp", axis=1, tiled=True),
        preferred_element_type=jnp.float32,
    )
    parts = product.astype(jnp.bfloat16) * switch
    chosen_out, filled_out = post_table(
        out_owner[mine], out_rank[mine], alive_mine, groups, capacity
    )
    arrived_parts = lax.all_to_all(
        pack_parts(parts, chosen_out, filled_out), "tensor", split_axis=1, concat_axis=1, tiled=True
    )
    mixed = (
        collect_parts(
            arrived_parts, out_owner, out_local, out_rank, alive, mine, capacity, per_device
        )
        + cross_bias
    )
    cross_out = (start_wide * mixed + start_wide).astype(jnp.bfloat16)
    whole_grad = lax.all_gather(grad_mixed_low, "tensor", axis=1, tiled=True)
    upstream = jnp.take(whole_grad.reshape(row_count, -1, BLK), out_blocks[mine], axis=1)
    upstream = upstream * switch
    backward = jnp.einsum(
        "rkj,kij->rki",
        upstream,
        lax.all_gather(cross_blocks, "dp", axis=1, tiled=True),
        preferred_element_type=jnp.float32,
    )
    back_parts = backward.astype(jnp.bfloat16)
    chosen_in, filled_in = post_table(in_owner[mine], in_rank[mine], alive_mine, groups, capacity)
    arrived_back = lax.all_to_all(
        pack_parts(back_parts, chosen_in, filled_in),
        "tensor",
        split_axis=1,
        concat_axis=1,
        tiled=True,
    )
    grad_start = collect_parts(
        arrived_back, in_owner, in_local, in_rank, alive, mine, capacity, per_device
    )
    block_terms = jnp.einsum("rki,rkj->kij", fetched, upstream, preferred_element_type=jnp.float32)
    grad_blocks = lax.psum_scatter(
        block_terms.astype(jnp.bfloat16), "dp", scatter_dimension=1, tiled=True
    ).astype(jnp.float32)
    grad_start = grad_start + cot_wide * mixed + cot_wide
    sigma = jax.nn.sigmoid(preact)
    grad_pre = grad_start * sigma * (1.0 + preact * (1.0 - sigma))
    grad_pre_low = grad_pre.astype(jnp.bfloat16)
    taken = dense
    grad_bottom = lax.psum_scatter(
        lax.dot_general(
            taken, grad_pre_low, (((0,), (0,)), ((), ())), preferred_element_type=jnp.float32
        ).astype(jnp.bfloat16),
        "dp",
        scatter_dimension=0,
        tiled=True,
    ).astype(jnp.float32)
    bias_sums = lax.psum((jnp.sum(grad_pre, axis=0), jnp.sum(grad_mixed, axis=0)), "dp")
    return (cross_out, grad_bottom, bias_sums[0], grad_blocks, bias_sums[1])


def solution(mesh):
    return jax.shard_map(
        on_device,
        mesh=mesh,
        in_specs=(
            P("dp", None),
            P(None, "tensor"),
            P("tensor"),
            P("tensor", "dp", None),
            P("tensor"),
            P("dp", "tensor"),
            P(),
            P(),
            P(),
        ),
        out_specs=(
            P("dp", "tensor"),
            P("dp", "tensor"),
            P("tensor"),
            P("tensor", "dp", None),
            P("tensor"),
        ),
        check_vma=False,
    )
```

profile of v0, /device:TPU:0, one launch (start us, length us, event | category | flops | bytes accessed | tf_op | source)
XLA Modules:
  0.0 400.9 jit_solution(8510571627176802936)
XLA Ops:
  8.3 7.8 %fusion.9 = (f32[2048]{0:T(1024)}, bf16[192,2048]{1,0:T(8,128)(2,1)}, f32[192,2048]{1,0:T(8,128)}) fusion(bf16[192,2048]{1,0:T(8,128)(2,1)} %param.18, f32[2048]{0:T(1024)} %param.15, bf16[192,2048]{1,0:T(8,128)(2,1)S(1)} %copy-done, bf16[2048,2048]{1,0:T(8,128)(2,1)} %param.14), kind=kOutput, calls=%fused_computation.28 | convolution fusion | flops 1614542848 | bytes 12337152 | tf_op jit(solution)/shard_map/dot_general | solution.py:72
  16.2 2.3 fusion.10
  21.2 38.5 %all-gather.4.cloned.1.call-done = bf16[192,16384]{1,0:T(8,128)(2,1)} async-done(((bf16[192,2048]{1,0:T(8,128)(2,1)}), bf16[192,16384]{1,0:T(8,128)(2,1)}) %all-gather.4.cloned.1.call-update) | async-done | bytes 6291472 | tf_op jit(solution)/shard_map/all_gather | solution.py:87
  59.6 6.2 %copy.90 = bf16[24,32,8,512]{3,2,0,1:T(8,128)(2,1)} copy(bf16[24,32,8,512]{3,2,1,0:T(8,128)(2,1)} %bitcast.71) | data formatting | bytes 12582912 | tf_op jit(solution)/shard_map/reshape | solution.py:88
  65.8 37.0 %all-gather.8.cloned.1.call-done = bf16[192,16384]{1,0:T(8,128)(2,1)} async-done(((bf16[192,2048]{1,0:T(8,128)(2,1)}), bf16[192,16384]{1,0:T(8,128)(2,1)}) %all-gather.8.cloned.1.call-update) | async-done | bytes 6291472 | tf_op jit(solution)/shard_map/all_gather | solution.py:110
  102.9 6.3 %copy.89 = bf16[24,32,8,512]{3,2,0,1:T(8,128)(2,1)} copy(bf16[24,32,8,512]{3,2,1,0:T(8,128)(2,1)} %bitcast.72) | data formatting | bytes 12582912 | tf_op jit(solution)/shard_map/reshape | solution.py:111
  109.2 4.9 %gather_fusion = bf16[10,192,512]{2,1,0:T(8,128)(2,1)} fusion(bf16[192,32,512]{2,0,1:T(8,128)(2,1)} %bitcast.69, s32[1024]{0:T(1024)S(1)} %pad_clamp_fusion.3), kind=kCustom, calls=%fused_computation.clone | custom fusion | bytes 3932200 | tf_op jit(solution)/shard_map/jit(_take)/gather | solution.py:88
  114.0 3.7 gather_fusion.2
  117.8 5.8 %convolution_convert_fusion = bf16[10,512,512]{2,1,0:T(8,128)(2,1)} fusion(bf16[10,192,512]{2,1,0:T(8,128)(2,1)} %gather_fusion, pred[10]{0:T(512)(128)(4,1)} %get-tuple-element.65, bf16[10,192,512]{2,1,0:T(8,128)(2,1)S(1)} %gather_fusion.2, pred[10]{0:T(512)(128)(4,1)S(1)} %get-tuple-element.44, bf16[10]{0:T(256)(128)(2,1)} %get-tuple-element.50), kind=kOutput, calls=%fused_computation.9 | convolution fusion | flops 1012203520 | bytes 9175080 | tf_op jit(solution)/shard_map/rki,rkj->kij/dot_general | solution.py:131
  127.7 1.4 fusion.14
  129.7 1.3 copy.61
  131.0 1.4 reshape.262
  132.4 1.5 select_reduce_fusion
  133.8 1.3 copy.59
  138.9 22.7 %all-gather.6.cloned.1.call-done = bf16[10,512,512]{2,1,0:T(8,128)(2,1)} async-done(((bf16[10,32,512]{2,1,0:T(8,128)(2,1)}), bf16[10,512,512]{2,1,0:T(8,128)(2,1)}) %all-gather.6.cloned.1.call-update) | async-done | bytes 5242896 | tf_op jit(solution)/shard_map/all_gather | solution.py:93
  161.6 5.7 %multiply_bitcast_fusion = bf16[192,10,512]{2,0,1:T(8,128)(2,1)} fusion(bf16[10,512,512]{2,1,0:T(8,128)(2,1)} %all-gather.6.cloned.1.call-done, bf16[10]{0:T(256)(128)(2,1)} %get-tuple-element.50, bf16[10,192,512]{2,1,0:T(8,128)(2,1)} %gather_fusion, pred[10]{0:T(512)(128)(4,1)} %get-tuple-element.65), kind=kOutput, calls=%fused_computation.20 | convolution fusion | flops 1009582080 | bytes 9175070 | tf_op jit(solution)/shard_map/rki,kij->rkj/dot_general | solution.py:90
  167.3 4.0 %gather_fusion.1 = bf16[16,192,512]{2,1,0:T(8,128)(2,1)} fusion(bf16[192,10,512]{2,0,1:T(8,128)(2,1)} %multiply_bitcast_fusion, s32[1024]{0:T(1024)} %pad_clamp_fusion.2), kind=kCustom, calls=%fused_computation.1.clone | custom fusion | bytes 6291520 | tf_op jit(solution)/shard_map/jit(_take)/gather | solution.py:30
  171.4 2.3 bitcast_multiply_fusion.1
  173.6 3.4 copy.62
  177.1 5.7 %reshape.254 = bf16[192,8,1024]{2,1,0:T(8,128)(2,1)} reshape(bf16[192,16,512]{2,1,0:T(8,128)(2,1)} %copy.62) | data formatting | bytes 6291456 | tf_op jit(solution)/shard_map/reshape | solution.py:33
  182.8 5.4 %copy.63 = bf16[192,8,1024]{2,0,1:T(8,128)(2,1)} copy(bf16[192,8,1024]{2,1,0:T(8,128)(2,1)} %reshape.254) | data formatting | bytes 6291456 | tf_op jit(solution)/shard_map/reshape | solution.py:33
  188.1 4.6 %all-to-all-start = ((bf16[192,8,1024]{2,0,1:T(8,128)(2,1)}), bf16[192,8,1024]{2,0,1:T(8,128)(2,1)}, u32[]{:S(2)}, u32[]{:S(2)}) async-start(bf16[192,8,1024]{2,0,1:T(8,128)(2,1)} %copy.63), calls=%async_computation | async-start | bytes 6291456 | tf_op jit(solution)/shard_map/all_to_all | solution.py:100
  193.9 1.3 copy.71
  195.2 1.4 reshape.263
  196.6 1.3 copy.69
  197.9 1.3 reshape.258
  201.6 5.8 %convert_bitcast_fusion.1 = bf16[192,10,512]{2,0,1:T(8,128)(2,1)} fusion(bf16[10,512,512]{2,1,0:T(8,128)(2,1)} %all-gather.6.cloned.1.call-done, bf16[10,192,512]{2,1,0:T(8,128)(2,1)S(1)} %gather_fusion.2, pred[10]{0:T(512)(128)(4,1)} %copy-done.21, bf16[10]{0:T(256)(128)(2,1)} %get-tuple-element.50), kind=kOutput, calls=%fused_computation.19 | convolution fusion | flops 1009582080 | bytes 9175070 | tf_op jit(solution)/shard_map/rkj,kij->rki/dot_general | solution.py:113
  207.4 4.1 %gather_fusion.3 = bf16[16,192,512]{2,1,0:T(8,128)(2,1)} fusion(bf16[192,10,512]{2,0,1:T(8,128)(2,1)} %convert_bitcast_fusion.1, s32[1024]{0:T(1024)} %pad_clamp_fusion), kind=kCustom, calls=%fused_computation.3.clone | custom fusion | bytes 6291520 | tf_op jit(solution)/shard_map/jit(_take)/gather | solution.py:30
  211.6 2.3 bitcast_multiply_fusion
  213.8 3.5 copy.72
  217.3 5.7 %reshape.259 = bf16[192,8,1024]{2,1,0:T(8,128)(2,1)} reshape(bf16[192,16,512]{2,1,0:T(8,128)(2,1)} %copy.72) | data formatting | bytes 6291456 | tf_op jit(solution)/shard_map/reshape | solution.py:33
  223.0 5.3 %copy.73 = bf16[192,8,1024]{2,0,1:T(8,128)(2,1)} copy(bf16[192,8,1024]{2,1,0:T(8,128)(2,1)} %reshape.259) | data formatting | bytes 6291456 | tf_op jit(solution)/shard_map/reshape | solution.py:33
  228.3 2.9 all-to-all-done
  231.2 4.4 %all-to-all-start.1 = ((bf16[192,8,1024]{2,0,1:T(8,128)(2,1)}), bf16[192,8,1024]{2,0,1:T(8,128)(2,1)}, u32[]{:S(2)}, u32[]{:S(2)}) async-start(bf16[192,8,1024]{2,0,1:T(8,128)(2,1)} %copy.73), calls=%async_computation.1 | async-start | bytes 6291456 | tf_op jit(solution)/shard_map/all_to_all | solution.py:121
  236.6 5.3 %copy.64 = bf16[192,8,1024]{2,1,0:T(8,128)(2,1)} copy(bf16[192,8,1024]{2,0,1:T(8,128)(2,1)} %all-to-all-done) | data formatting | bytes 6291456 | tf_op jit(solution)/shard_map/all_to_all | solution.py:100
  241.9 5.7 %reshape.255 = bf16[192,16,512]{2,1,0:T(8,128)(2,1)} reshape(bf16[192,8,1024]{2,1,0:T(8,128)(2,1)} %copy.64) | data formatting | bytes 6291456 | tf_op jit(solution)/shard_map/reshape | solution.py:50
  247.6 2.5 fusion.29
  250.7 23.4 %all-to-all-done.1 = bf16[192,8,1024]{2,0,1:T(8,128)(2,1)} async-done(((bf16[192,8,1024]{2,0,1:T(8,128)(2,1)}), bf16[192,8,1024]{2,0,1:T(8,128)(2,1)}, u32[]{:S(2)}, u32[]{:S(2)}) %all-to-all-start.1) | async-done | bytes 3145760 | tf_op jit(solution)/shard_map/all_to_all | solution.py:121
  274.0 5.2 %copy.74 = bf16[192,8,1024]{2,1,0:T(8,128)(2,1)} copy(bf16[192,8,1024]{2,0,1:T(8,128)(2,1)} %all-to-all-done.1) | data formatting | bytes 6291456 | tf_op jit(solution)/shard_map/all_to_all | solution.py:121
  279.3 5.6 %reshape.260 = bf16[192,16,512]{2,1,0:T(8,128)(2,1)} reshape(bf16[192,8,1024]{2,1,0:T(8,128)(2,1)} %copy.74) | data formatting | bytes 6291456 | tf_op jit(solution)/shard_map/reshape | solution.py:50
  284.9 2.5 fusion.30
  289.1 1.9 fusion.26
  290.9 5.6 %convert_bitcast_fusion = bf16[2048,2048]{0,1:T(8,128)(2,1)} fusion(bf16[192,2048]{1,0:T(8,128)(2,1)S(1)} %copy-done, bf16[192,2048]{1,0:T(8,128)(2,1)S(1)} %get-tuple-element.43), kind=kOutput, calls=%fused_computation.4 | convolution fusion | flops 1614807040 | bytes 9961472 | tf_op jit(solution)/shard_map/dot_general | solution.py:141
  296.6 12.3 %copy.81 = bf16[2048,2048]{1,0:T(8,128)(2,1)} copy(bf16[2048,2048]{0,1:T(8,128)(2,1)} %convert_bitcast_fusion) | data formatting | bytes 16777216
  309.5 72.9 %all-reduce = (f32[2048]{0:T(1024)}, f32[2048]{0:T(1024)}) all-reduce(f32[2048]{0:T(1024)S(1)} %get-tuple-element.42, f32[2048]{0:T(1024)S(1)} %copy-done.10), channel_id=1, replica_groups=mesh['dp'=16,'tensor'=8] {'dp'}, use_global_device_ids=true, to_apply=%region_10.13 | all-reduce | flops 4096 | bytes 32768 | tf_op jit(solution)/shard_map/psum | solution.py:148
  382.4 1.9 convert_element_type.136
  384.3 7.5 %reduce-scatter.7.cloned.1.call-done = bf16[128,2048]{1,0:T(8,128)(2,1)} async-done(((bf16[2048,2048]{1,0:T(8,128)(2,1)}), bf16[128,2048]{1,0:T(8,128)(2,1)}) %reduce-scatter.7.cloned.1.call-update) | async-done | bytes 524304
  391.8 1.3 copy.82
  (97 shorter events, 20.8 us)
Async XLA Ops:
  7.2 1.1 copy-start
  7.2 9.0 %copy-start.2 = (bf16[192,2048]{1,0:T(8,128)(2,1)S(1)}, bf16[192,2048]{1,0:T(8,128)(2,1)}, u32[]{:S(2)}) copy-start(bf16[192,2048]{1,0:T(8,128)(2,1)} %param.18) | copy-start | bytes 2359300
  7.2 52.4 %all-gather.4.cloned.1.call-start = ((), (), s32[]{:S(2)}) async-start(), calls=%async_computation.4 | async-start | bytes 7077888 | tf_op jit(solution)/shard_map/all_gather | solution.py:87
  16.1 3.2 copy-start.6
  16.1 3.2 copy-start.8
  16.1 3.2 copy-start.20
  16.1 86.8 %all-gather.8.cloned.1.call-start = ((), (), s32[]{:S(2)}) async-start(), calls=%async_computation.6 | async-start | bytes 7077888 | tf_op jit(solution)/shard_map/all_gather | solution.py:110
  18.5 143.1 %all-gather.6.cloned.1.call-start = ((), (), s32[]{:S(2)}) async-start(), calls=%async_computation.5 | async-start | bytes 5570560 | tf_op jit(solution)/shard_map/all_gather | solution.py:93
  19.2 363.2 %reduce-scatter.5.cloned.1.call-start = ((), (), s32[]{:S(2)}) async-start(), calls=%async_computation.7 | async-start | bytes 5570560 | tf_op jit(solution)/shard_map/reduce_scatter | solution.py:132
  20.0 45.9 %copy-start.12 = (pred[8,10]{1,0:T(8,128)(4,1)}, pred[8,10]{1,0:T(8,128)(4,1)S(1)}, u32[]{:S(2)}) copy-start(pred[8,10]{1,0:T(8,128)(4,1)S(1)} %get-tuple-element.57) | copy-start | bytes 244
  20.0 103.6 %copy-start.4 = (s32[8,10]{1,0:T(8,128)}, s32[8,10]{1,0:T(8,128)S(1)}, u32[]{:S(2)}) copy-start(s32[8,10]{1,0:T(8,128)S(1)} %get-tuple-element.53) | copy-start | bytes 964
  20.0 104.3 %copy-start.5 = (s32[8,10]{1,0:T(8,128)}, s32[8,10]{1,0:T(8,128)S(1)}, u32[]{:S(2)}) copy-start(s32[8,10]{1,0:T(8,128)S(1)} %get-tuple-element.56) | copy-start | bytes 964
  21.1 96.6 %copy-start.21 = (pred[10]{0:T(512)(128)(4,1)}, pred[10]{0:T(512)(128)(4,1)S(1)}, u32[]{:S(2)}) copy-start(pred[10]{0:T(512)(128)(4,1)S(1)} %get-tuple-element.44) | copy-start | bytes 34
  127.1 2.0 copy-start.17
  127.1 2.0 copy-start.18
  127.1 0.6 copy-start.15
  127.2 1.9 copy-start.16
  188.1 43.1 %all-to-all-start = ((bf16[192,8,1024]{2,0,1:T(8,128)(2,1)}), bf16[192,8,1024]{2,0,1:T(8,128)(2,1)}, u32[]{:S(2)}, u32[]{:S(2)}) async-start(bf16[192,8,1024]{2,0,1:T(8,128)(2,1)} %copy.63), calls=%async_computation | async-start | bytes 6291456 | tf_op jit(solution)/shard_map/all_to_all | solution.py:100
  207.4 4.2 %copy-start.19 = (bf16[16]{0:T(256)(128)(2,1)S(1)}, bf16[16]{0:T(256)(128)(2,1)}, u32[]{:S(2)}) copy-start(bf16[16]{0:T(256)(128)(2,1)} %reshape.263) | copy-start | bytes 100
  207.4 4.2 %copy-start.22 = (pred[16]{0:T(512)(128)(4,1)S(1)}, pred[16]{0:T(512)(128)(4,1)}, u32[]{:S(2)}) copy-start(pred[16]{0:T(512)(128)(4,1)} %compare_and_fusion.2) | copy-start | bytes 52
  228.3 7.5 %copy-start.7 = (s32[8,10]{1,0:T(8,128)S(1)}, s32[8,10]{1,0:T(8,128)}, u32[]{:S(2)}) copy-start(s32[8,10]{1,0:T(8,128)} %param.20) | copy-start | bytes 964
  228.3 7.5 %copy-start.13 = (pred[8,10]{1,0:T(8,128)(4,1)S(1)}, pred[8,10]{1,0:T(8,128)(4,1)}, u32[]{:S(2)}) copy-start(pred[8,10]{1,0:T(8,128)(4,1)} %get-tuple-element.52) | copy-start | bytes 244
  228.3 7.6 %copy-start.14 = (pred[8,10]{1,0:T(8,128)(4,1)S(1)}, pred[8,10]{1,0:T(8,128)(4,1)}, u32[]{:S(2)}) copy-start(pred[8,10]{1,0:T(8,128)(4,1)} %get-tuple-element.55) | copy-start | bytes 244
  228.3 7.8 %copy-start.9 = (s32[8,10]{1,0:T(8,128)S(1)}, s32[8,10]{1,0:T(8,128)}, u32[]{:S(2)}) copy-start(s32[8,10]{1,0:T(8,128)} %param.19) | copy-start | bytes 964
  231.2 42.9 %all-to-all-start.1 = ((bf16[192,8,1024]{2,0,1:T(8,128)(2,1)}), bf16[192,8,1024]{2,0,1:T(8,128)(2,1)}, u32[]{:S(2)}, u32[]{:S(2)}) async-start(bf16[192,8,1024]{2,0,1:T(8,128)(2,1)} %copy.73), calls=%async_computation.1 | async-start | bytes 6291456 | tf_op jit(solution)/shard_map/all_to_all | solution.py:121
  235.6 156.2 %reduce-scatter.7.cloned.1.call-start = ((), (), s32[]{:S(2)}) async-start(), calls=%async_computation.8 | async-start | bytes 8912896
  287.4 1.1 copy-start.1
  287.4 1.6 copy-start.3
  287.5 1.6 copy-start.11
  308.8 0.7 copy-start.10
Sparse Core Ops, SparseCore 0:
  16.3 43.3 all-gather.3
  61.9 40.9 all-gather.7
  105.0 56.5 all-gather.5
  164.9 78.7 reduce-scatter.4
  309.0 82.7 reduce-scatter.6
where the time goes:
time: 403 us; the launch traced here: 401 us
  waiting for transfers between devices  133 us (33%)
  local copies, waits for them, and re-layouts  113 us (28%)
  blocking collectives  72.9 us (18%)
  matrix products  35.7 us (9%)
  other arithmetic  23.6 us (6%)
  between operations  14.1 us (3%)
  starting transfers between devices  9.25 us (2%)
    psum x1, blocking collectives, on_device(): lax.psum((jnp.sum(grad_pre, axis=0), jnp.sum(grad_mixed, axis=0)), 'dp')  72.9 us
    all_gather x1, waiting for transfers between devices, on_device(): whole_start = lax.all_gather(start, 'tensor', axis=1, tiled=True)  38.5 us
    all_gather x1, waiting for transfers between devices, on_device(): whole_grad = lax.all_gather(grad_mixed_low, 'tensor', axis=1, tiled=True)  37 us
    all_to_all x1, waiting for transfers between devices, on_device(): lax.all_to_all(pack_parts(back_parts, chosen_in, filled_in), 'tensor', sp...  23.4 us
    all_gather x1, waiting for transfers between devices, on_device(): lax.all_gather(cross_blocks, 'dp', axis=1, tiled=True)  22.7 us
    reshape x4, local copies, waits for them, and re-layouts, pack_parts(): picked.reshape(parts.shape[0], chosen.shape[0], chosen.shape[1] * parts.s...  22.1 us
    unnamed x51, local copies, waits for them, and re-layouts  19.4 us
    reshape x2, local copies, waits for them, and re-layouts, collect_parts(): flattened = received.reshape(row_count, groups * capacity, block_width)  11.3 us
  transfers between devices with their start and end apart: 7, of which 6 were waited for; matrix products, arithmetic and copies ran while one was open for 39% of the time, Pallas kernels for 0%

commit v1 on v0

--- a/solution.py
+++ b/solution.py
@@ -2,9 +2,19 @@
 import jax.numpy as jnp
 from jax import lax
 from jax.sharding import PartitionSpec as P
+from jax.lax import all_to_all, axis_size
 
 BLK = 512
 SLOTS = 10
+
+
+def sectors_load(inp):
+    buffers = []
+    for _ in range(axis_size("dp")):
+        buffers.append(inp)
+    row_out = jnp.stack(buffers, axis=0)
+    upper = all_to_all(row_out, "dp", 0, 0)
+    return jnp.concatenate(upper, 1)
 
 
 def slot_ranks(owner, alive):
@@ -88,10 +98,7 @@
     fetched = jnp.take(whole_start.reshape(row_count, -1, BLK), in_blocks[mine], axis=1)
     taken = fetched
     product = jnp.einsum(
-        "rki,kij->rkj",
-        taken,
-        lax.all_gather(cross_blocks, "dp", axis=1, tiled=True),
-        preferred_element_type=jnp.float32,
+        "rki,kij->rkj", taken, sectors_load(cross_blocks), preferred_element_type=jnp.float32
     )
     parts = product.astype(jnp.bfloat16) * switch
     chosen_out, filled_out = post_table(

time: 403 us -> 382 us (0.948)
  waiting for transfers between devices: 133 us -> 97.5 us
  starting transfers between devices: 9.25 us -> 18.1 us
  local copies, waits for them, and re-layouts: 113 us -> 119 us
    all_gather x1, waiting for transfers between devices: 22.7 us -> 0.01 us  [on_device(): lax.all_gather(cross_blocks, 'dp', axis=1, tiled=True)]
    all_gather x1, waiting for transfers between devices: 38.5 us -> 26.9 us  [on_device(): whole_start = lax.all_gather(start, 'tensor', axis=1, tiled=True)]
    all_to_all x0 -> x1, starting transfers between devices: none -> 8.31 us  [sectors_load(): upper = all_to_all(row_out, 'dp', 0, 0)]
    unnamed x51 -> x59, local copies, waits for them, and re-layouts: 19.4 us -> 19.3 us
  transfers between devices with their start and end apart: 7 -> 8, of which waited for: 6 -> 5; matrix products, arithmetic and copies ran while one was open for 39% -> 42% of each run, Pallas kernels for 0% -> 0%
where the time goes in v1:
time: 382 us; the launch traced here: 379 us
  local copies, waits for them, and re-layouts  119 us (31%)
  waiting for transfers between devices  97.5 us (26%)
  blocking collectives  75.2 us (20%)
  matrix products  32.6 us (9%)
  other arithmetic  23.3 us (6%)
  starting transfers between devices  18.1 us (5%)
  between operations  14.1 us (4%)
    psum x1, blocking collectives, on_device(): lax.psum((jnp.sum(grad_pre, axis=0), jnp.sum(grad_mixed, axis=0)), 'dp')  75.2 us
    all_gather x1, waiting for transfers between devices, on_device(): whole_grad = lax.all_gather(grad_mixed_low, 'tensor', axis=1, tiled=True)  37 us
    all_gather x1, waiting for transfers between devices, on_device(): whole_start = lax.all_gather(start, 'tensor', axis=1, tiled=True)  26.9 us
    all_to_all x1, waiting for transfers between devices, on_device(): lax.all_to_all(pack_parts(back_parts, chosen_in, filled_in), 'tensor', sp...  23.1 us
    reshape x4, local copies, waits for them, and re-layouts, pack_parts(): picked.reshape(parts.shape[0], chosen.shape[0], chosen.shape[1] * parts.s...  22.1 us
    unnamed x59, local copies, waits for them, and re-layouts  19.3 us
    reshape x2, local copies, waits for them, and re-layouts, collect_parts(): flattened = received.reshape(row_count, groups * capacity, block_width)  11.3 us
    all_to_all x1, starting transfers between devices, sectors_load(): upper = all_to_all(row_out, 'dp', 0, 0)  8.31 us
  transfers between devices with their start and end apart: 8, of which 5 were waited for; matrix products, arithmetic and copies ran while one was open for 42% of the time, Pallas kernels for 0%

profile of v1, /device:TPU:0, one launch (start us, length us, event | category | flops | bytes accessed | tf_op | source)
XLA Modules:
  0.0 379.5 jit_solution(15094301369606145670)
XLA Ops:
  8.3 7.8 %fusion.9 = (f32[2048]{0:T(1024)}, bf16[192,2048]{1,0:T(8,128)(2,1)}, f32[192,2048]{1,0:T(8,128)}) fusion(bf16[192,2048]{1,0:T(8,128)(2,1)} %param.18, f32[2048]{0:T(1024)} %param.15, bf16[192,2048]{1,0:T(8,128)(2,1)S(1)} %copy-done, bf16[2048,2048]{1,0:T(8,128)(2,1)} %param.14), kind=kOutput, calls=%fused_computation.28 | convolution fusion | flops 1614542848 | bytes 12337152 | tf_op jit(solution)/shard_map/dot_general | solution.py:82
  16.2 2.3 fusion.10
  19.3 3.1 stack.2
  22.3 8.3 %all-to-all-start = ((bf16[16,10,32,512]{3,2,1,0:T(8,128)(2,1)}), bf16[16,10,32,512]{3,2,1,0:T(8,128)(2,1)}, u32[]{:S(2)}, u32[]{:S(2)}) async-start(bf16[16,10,32,512]{3,2,1,0:T(8,128)(2,1)} %stack.2), calls=%async_computation | async-start | bytes 10485760 | tf_op jit(solution)/shard_map/all_to_all | solution.py:16
  32.7 26.9 %all-gather.4.cloned.1.call-done = bf16[192,16384]{1,0:T(8,128)(2,1)} async-done(((bf16[192,2048]{1,0:T(8,128)(2,1)}), bf16[192,16384]{1,0:T(8,128)(2,1)}) %all-gather.4.cloned.1.call-update) | async-done | bytes 6291472 | tf_op jit(solution)/shard_map/all_gather | solution.py:97
  59.6 6.2 %copy.93 = bf16[24,32,8,512]{3,2,0,1:T(8,128)(2,1)} copy(bf16[24,32,8,512]{3,2,1,0:T(8,128)(2,1)} %bitcast.73) | data formatting | bytes 12582912 | tf_op jit(solution)/shard_map/reshape | solution.py:98
  65.8 37.0 %all-gather.6.cloned.1.call-done = bf16[192,16384]{1,0:T(8,128)(2,1)} async-done(((bf16[192,2048]{1,0:T(8,128)(2,1)}), bf16[192,16384]{1,0:T(8,128)(2,1)}) %all-gather.6.cloned.1.call-update) | async-done | bytes 6291472 | tf_op jit(solution)/shard_map/all_gather | solution.py:117
  102.9 6.3 %copy.92 = bf16[24,32,8,512]{3,2,0,1:T(8,128)(2,1)} copy(bf16[24,32,8,512]{3,2,1,0:T(8,128)(2,1)} %bitcast.74) | data formatting | bytes 12582912 | tf_op jit(solution)/shard_map/reshape | solution.py:118
  109.1 4.9 %gather_fusion = bf16[10,192,512]{2,1,0:T(8,128)(2,1)} fusion(bf16[192,32,512]{2,0,1:T(8,128)(2,1)} %bitcast.71, s32[1024]{0:T(1024)S(1)} %pad_clamp_fusion.3), kind=kCustom, calls=%fused_computation.clone | custom fusion | bytes 3932200 | tf_op jit(solution)/shard_map/jit(_take)/gather | solution.py:98
  114.0 3.7 gather_fusion.2
  117.7 5.8 %convolution_convert_fusion = bf16[10,512,512]{2,1,0:T(8,128)(2,1)} fusion(bf16[10,192,512]{2,1,0:T(8,128)(2,1)} %gather_fusion, pred[10]{0:T(512)(128)(4,1)} %get-tuple-element.48, bf16[10,192,512]{2,1,0:T(8,128)(2,1)S(1)} %gather_fusion.2, pred[10]{0:T(512)(128)(4,1)S(1)} %get-tuple-element.44, bf16[10]{0:T(256)(128)(2,1)} %get-tuple-element.50), kind=kOutput, calls=%fused_computation.9 | convolution fusion | flops 1012203520 | bytes 9175080 | tf_op jit(solution)/shard_map/rki,rkj->kij/dot_general | solution.py:138
  127.7 1.3 select_reduce_fusion
  129.0 1.3 copy.61
  130.3 1.3 reshape.263
  131.6 1.3 fusion.14
  133.5 1.3 copy.64
  138.4 3.1 copy.63
  141.5 2.6 multiply_bitcast_fusion
  144.1 4.1 %gather_fusion.1 = bf16[16,192,512]{2,1,0:T(8,128)(2,1)} fusion(bf16[192,10,512]{2,0,1:T(8,128)(2,1)} %multiply_bitcast_fusion, s32[1024]{0:T(1024)} %pad_clamp_fusion.2), kind=kCustom, calls=%fused_computation.1.clone | custom fusion | bytes 6291520 | tf_op jit(solution)/shard_map/jit(_take)/gather | solution.py:40
  148.2 2.3 bitcast_multiply_fusion.1
  150.5 3.4 copy.65
  154.0 5.7 %reshape.264 = bf16[192,8,1024]{2,1,0:T(8,128)(2,1)} reshape(bf16[192,16,512]{2,1,0:T(8,128)(2,1)} %copy.65) | data formatting | bytes 6291456 | tf_op jit(solution)/shard_map/reshape | solution.py:43
  159.7 5.3 %copy.66 = bf16[192,8,1024]{2,0,1:T(8,128)(2,1)} copy(bf16[192,8,1024]{2,1,0:T(8,128)(2,1)} %reshape.264) | data formatting | bytes 6291456 | tf_op jit(solution)/shard_map/reshape | solution.py:43
  165.0 4.7 %all-to-all-start.1 = ((bf16[192,8,1024]{2,0,1:T(8,128)(2,1)}), bf16[192,8,1024]{2,0,1:T(8,128)(2,1)}, u32[]{:S(2)}, u32[]{:S(2)}) async-start(bf16[192,8,1024]{2,0,1:T(8,128)(2,1)} %copy.66), calls=%async_computation.1 | async-start | bytes 6291456 | tf_op jit(solution)/shard_map/all_to_all | solution.py:107
  169.6 1.3 copy.72
  174.7 1.3 reshape.273
  178.4 5.8 %convert_bitcast_fusion.1 = bf16[192,10,512]{2,0,1:T(8,128)(2,1)} fusion(bf16[10,512,512]{2,1,0:T(8,128)(2,1)} %all-gather.8.cloned.1.call-done, bf16[10,192,512]{2,1,0:T(8,128)(2,1)S(1)} %gather_fusion.2, pred[10]{0:T(512)(128)(4,1)} %copy-done.23, bf16[10]{0:T(256)(128)(2,1)} %get-tuple-element.50), kind=kOutput, calls=%fused_computation.19 | convolution fusion | flops 1009582080 | bytes 9175070 | tf_op jit(solution)/shard_map/rkj,kij->rki/dot_general | solution.py:120
  184.2 4.2 %gather_fusion.3 = bf16[16,192,512]{2,1,0:T(8,128)(2,1)} fusion(bf16[192,10,512]{2,0,1:T(8,128)(2,1)} %convert_bitcast_fusion.1, s32[1024]{0:T(1024)} %pad_clamp_fusion), kind=kCustom, calls=%fused_computation.3.clone | custom fusion | bytes 6291520 | tf_op jit(solution)/shard_map/jit(_take)/gather | solution.py:40
  188.4 2.3 bitcast_multiply_fusion
  190.6 3.5 copy.75
  194.1 5.7 %reshape.269 = bf16[192,8,1024]{2,1,0:T(8,128)(2,1)} reshape(bf16[192,16,512]{2,1,0:T(8,128)(2,1)} %copy.75) | data formatting | bytes 6291456 | tf_op jit(solution)/shard_map/reshape | solution.py:43
  199.8 5.4 %copy.76 = bf16[192,8,1024]{2,0,1:T(8,128)(2,1)} copy(bf16[192,8,1024]{2,1,0:T(8,128)(2,1)} %reshape.269) | data formatting | bytes 6291456 | tf_op jit(solution)/shard_map/reshape | solution.py:43
  205.2 2.7 all-to-all-done.1
  207.9 4.5 %all-to-all-start.2 = ((bf16[192,8,1024]{2,0,1:T(8,128)(2,1)}), bf16[192,8,1024]{2,0,1:T(8,128)(2,1)}, u32[]{:S(2)}, u32[]{:S(2)}) async-start(bf16[192,8,1024]{2,0,1:T(8,128)(2,1)} %copy.76), calls=%async_computation.2 | async-start | bytes 6291456 | tf_op jit(solution)/shard_map/all_to_all | solution.py:128
  213.6 5.3 %copy.67 = bf16[192,8,1024]{2,1,0:T(8,128)(2,1)} copy(bf16[192,8,1024]{2,0,1:T(8,128)(2,1)} %all-to-all-done.1) | data formatting | bytes 6291456 | tf_op jit(solution)/shard_map/all_to_all | solution.py:107
  218.9 5.7 %reshape.265 = bf16[192,16,512]{2,1,0:T(8,128)(2,1)} reshape(bf16[192,8,1024]{2,1,0:T(8,128)(2,1)} %copy.67) | data formatting | bytes 6291456 | tf_op jit(solution)/shard_map/reshape | solution.py:60
  224.6 2.5 fusion.29
  227.7 23.1 %all-to-all-done.2 = bf16[192,8,1024]{2,0,1:T(8,128)(2,1)} async-done(((bf16[192,8,1024]{2,0,1:T(8,128)(2,1)}), bf16[192,8,1024]{2,0,1:T(8,128)(2,1)}, u32[]{:S(2)}, u32[]{:S(2)}) %all-to-all-start.2) | async-done | bytes 3145760 | tf_op jit(solution)/shard_map/all_to_all | solution.py:128
  250.8 5.3 %copy.77 = bf16[192,8,1024]{2,1,0:T(8,128)(2,1)} copy(bf16[192,8,1024]{2,0,1:T(8,128)(2,1)} %all-to-all-done.2) | data formatting | bytes 6291456 | tf_op jit(solution)/shard_map/all_to_all | solution.py:128
  256.0 5.7 %reshape.270 = bf16[192,16,512]{2,1,0:T(8,128)(2,1)} reshape(bf16[192,8,1024]{2,1,0:T(8,128)(2,1)} %copy.77) | data formatting | bytes 6291456 | tf_op jit(solution)/shard_map/reshape | solution.py:60
  261.7 2.5 fusion.30
  265.9 1.9 fusion.26
  267.7 5.6 %convert_bitcast_fusion = bf16[2048,2048]{0,1:T(8,128)(2,1)} fusion(bf16[192,2048]{1,0:T(8,128)(2,1)S(1)} %copy-done, bf16[192,2048]{1,0:T(8,128)(2,1)S(1)} %get-tuple-element.43), kind=kOutput, calls=%fused_computation.4 | convolution fusion | flops 1614807040 | bytes 9961472 | tf_op jit(solution)/shard_map/dot_general | solution.py:148
  273.4 12.2 %copy.84 = bf16[2048,2048]{1,0:T(8,128)(2,1)} copy(bf16[2048,2048]{0,1:T(8,128)(2,1)} %convert_bitcast_fusion) | data formatting | bytes 16777216
  286.2 75.2 %all-reduce = (f32[2048]{0:T(1024)}, f32[2048]{0:T(1024)}) all-reduce(f32[2048]{0:T(1024)S(1)} %get-tuple-element.42, f32[2048]{0:T(1024)S(1)} %copy-done.12), channel_id=1, replica_groups=mesh['dp'=16,'tensor'=8] {'dp'}, use_global_device_ids=true, to_apply=%region_10.13 | all-reduce | flops 4096 | bytes 32768 | tf_op jit(solution)/shard_map/psum | solution.py:155
  361.4 1.9 convert_element_type.136
  363.3 7.1 %reduce-scatter.7.cloned.1.call-done = bf16[128,2048]{1,0:T(8,128)(2,1)} async-done(((bf16[2048,2048]{1,0:T(8,128)(2,1)}), bf16[128,2048]{1,0:T(8,128)(2,1)}) %reduce-scatter.7.cloned.1.call-update) | async-done | bytes 524304
  370.4 1.3 copy.85
  (110 shorter events, 23.6 us)
Async XLA Ops:
  7.2 1.1 copy-start
  7.2 9.0 %copy-start.3 = (bf16[192,2048]{1,0:T(8,128)(2,1)S(1)}, bf16[192,2048]{1,0:T(8,128)(2,1)}, u32[]{:S(2)}) copy-start(bf16[192,2048]{1,0:T(8,128)(2,1)} %param.18) | copy-start | bytes 2359300
  7.2 52.4 %all-gather.4.cloned.1.call-start = ((), (), s32[]{:S(2)}) async-start(), calls=%async_computation.5 | async-start | bytes 7077888 | tf_op jit(solution)/shard_map/all_gather | solution.py:97
  16.1 3.2 copy-start.5
  16.1 86.8 %all-gather.6.cloned.1.call-start = ((), (), s32[]{:S(2)}) async-start(), calls=%async_computation.6 | async-start | bytes 7077888 | tf_op jit(solution)/shard_map/all_gather | solution.py:117
  18.5 159.9 %all-gather.8.cloned.1.call-start = ((), (), s32[]{:S(2)}) async-start(), calls=%async_computation.7 | async-start | bytes 5570560 | tf_op jit(solution)/shard_map/all_gather | solution.py:123
  22.3 8.6 %copy-start.10 = (s32[8,10]{1,0:T(8,128)S(1)}, s32[8,10]{1,0:T(8,128)}, u32[]{:S(2)}) copy-start(s32[8,10]{1,0:T(8,128)} %param.19) | copy-start | bytes 964
  22.3 9.1 %copy-start.8 = (s32[8,10]{1,0:T(8,128)S(1)}, s32[8,10]{1,0:T(8,128)}, u32[]{:S(2)}) copy-start(s32[8,10]{1,0:T(8,128)} %param.20) | copy-start | bytes 964
  22.3 9.1 %copy-start.22 = (s32[8]{0:T(128)S(1)}, s32[8]{0:T(128)}, u32[]{:S(2)}) copy-start(s32[8]{0:T(128)} %param.21) | copy-start | bytes 100
  22.3 116.1 %all-to-all-start = ((bf16[16,10,32,512]{3,2,1,0:T(8,128)(2,1)}), bf16[16,10,32,512]{3,2,1,0:T(8,128)(2,1)}, u32[]{:S(2)}, u32[]{:S(2)}) async-start(bf16[16,10,32,512]{3,2,1,0:T(8,128)(2,1)} %stack.2), calls=%async_computation | async-start | bytes 10485760 | tf_op jit(solution)/shard_map/all_to_all | solution.py:16
  30.7 330.8 %reduce-scatter.5.cloned.1.call-start = ((), (), s32[]{:S(2)}) async-start(), calls=%async_computation.8 | async-start | bytes 5570560 | tf_op jit(solution)/shard_map/reduce_scatter | solution.py:139
  31.5 86.3 %copy-start.23 = (pred[10]{0:T(512)(128)(4,1)}, pred[10]{0:T(512)(128)(4,1)S(1)}, u32[]{:S(2)}) copy-start(pred[10]{0:T(512)(128)(4,1)S(1)} %get-tuple-element.44) | copy-start | bytes 34
  32.1 33.8 %copy-start.14 = (pred[8,10]{1,0:T(8,128)(4,1)}, pred[8,10]{1,0:T(8,128)(4,1)S(1)}, u32[]{:S(2)}) copy-start(pred[8,10]{1,0:T(8,128)(4,1)S(1)} %get-tuple-element.57) | copy-start | bytes 244
  32.1 91.5 %copy-start.6 = (s32[8,10]{1,0:T(8,128)}, s32[8,10]{1,0:T(8,128)S(1)}, u32[]{:S(2)}) copy-start(s32[8,10]{1,0:T(8,128)S(1)} %get-tuple-element.53) | copy-start | bytes 964
  32.1 92.2 %copy-start.7 = (s32[8,10]{1,0:T(8,128)}, s32[8,10]{1,0:T(8,128)S(1)}, u32[]{:S(2)}) copy-start(s32[8,10]{1,0:T(8,128)S(1)} %get-tuple-element.56) | copy-start | bytes 964
  127.1 1.9 copy-start.19
  127.1 1.9 copy-start.20
  127.1 0.5 copy-start.17
  127.2 1.8 copy-start.18
  138.4 3.1 copy-start.2
  138.4 3.1 copy-start.24
  138.4 3.1 copy-start.25
  165.0 42.9 %all-to-all-start.1 = ((bf16[192,8,1024]{2,0,1:T(8,128)(2,1)}), bf16[192,8,1024]{2,0,1:T(8,128)(2,1)}, u32[]{:S(2)}, u32[]{:S(2)}) async-start(bf16[192,8,1024]{2,0,1:T(8,128)(2,1)} %copy.66), calls=%async_computation.1 | async-start | bytes 6291456 | tf_op jit(solution)/shard_map/all_to_all | solution.py:107
  184.2 4.2 %copy-start.21 = (bf16[16]{0:T(256)(128)(2,1)S(1)}, bf16[16]{0:T(256)(128)(2,1)}, u32[]{:S(2)}) copy-start(bf16[16]{0:T(256)(128)(2,1)} %reshape.273) | copy-start | bytes 100
  184.2 4.2 %copy-start.26 = (pred[16]{0:T(512)(128)(4,1)S(1)}, pred[16]{0:T(512)(128)(4,1)}, u32[]{:S(2)}) copy-start(pred[16]{0:T(512)(128)(4,1)} %compare_and_fusion.2) | copy-start | bytes 52
  205.2 7.6 %copy-start.9 = (s32[8,10]{1,0:T(8,128)S(1)}, s32[8,10]{1,0:T(8,128)}, u32[]{:S(2)}) copy-start(s32[8,10]{1,0:T(8,128)} %param.20) | copy-start | bytes 964
  205.2 7.6 %copy-start.15 = (pred[8,10]{1,0:T(8,128)(4,1)S(1)}, pred[8,10]{1,0:T(8,128)(4,1)}, u32[]{:S(2)}) copy-start(pred[8,10]{1,0:T(8,128)(4,1)} %get-tuple-element.52) | copy-start | bytes 244
  205.2 7.7 %copy-start.16 = (pred[8,10]{1,0:T(8,128)(4,1)S(1)}, pred[8,10]{1,0:T(8,128)(4,1)}, u32[]{:S(2)}) copy-start(pred[8,10]{1,0:T(8,128)(4,1)} %get-tuple-element.55) | copy-start | bytes 244
  205.2 8.0 %copy-start.11 = (s32[8,10]{1,0:T(8,128)S(1)}, s32[8,10]{1,0:T(8,128)}, u32[]{:S(2)}) copy-start(s32[8,10]{1,0:T(8,128)} %param.19) | copy-start | bytes 964
  207.9 42.9 %all-to-all-start.2 = ((bf16[192,8,1024]{2,0,1:T(8,128)(2,1)}), bf16[192,8,1024]{2,0,1:T(8,128)(2,1)}, u32[]{:S(2)}, u32[]{:S(2)}) async-start(bf16[192,8,1024]{2,0,1:T(8,128)(2,1)} %copy.76), calls=%async_computation.2 | async-start | bytes 6291456 | tf_op jit(solution)/shard_map/all_to_all | solution.py:128
  212.3 158.1 %reduce-scatter.7.cloned.1.call-start = ((), (), s32[]{:S(2)}) async-start(), calls=%async_computation.9 | async-start | bytes 8912896
  264.2 1.1 copy-start.1
  264.2 1.6 copy-start.4
  264.2 1.6 copy-start.13
  285.6 0.7 copy-start.12
Sparse Core Ops, SparseCore 0:
  16.2 43.3 all-gather.3
  61.9 40.9 all-gather.5
  105.0 56.5 all-gather.7
  164.9 78.6 reduce-scatter.4
  285.7 84.6 reduce-scatter.6
